TPU v7x, 32 devices: a whole 2x2x4 slice. The times are simulated.
32 devices in a mesh: twin: 2 (over x), dp: 16 (over z, y, core).
Axes of the slice: x: 2, y: 2, z: 4, core: 2. Of those that a mesh axis runs over, the one named last changes fastest.
Arguments:
- hidden: bfloat16 [64, 512, 768], P(('twin', 'dp')), may hold values from -6 to 6
- segment_ids: int32 [64, 512], P(('twin', 'dp')), may hold values from 0 to 7, never falling along the last dimension, each value on 1 to 128 neighbouring positions
- targets: int32 [256], replicated, may hold values from 0 to 255, each once
- w_qkv: bfloat16 [768, 2304], replicated, may hold values from -0.21875 to 0.21875
- b_query: bfloat16 [768], replicated, may hold values from -3 to 3
- b_value: bfloat16 [768], replicated, may hold values from -3 to 3
- w_out: bfloat16 [768, 768], replicated, may hold values from -1.25 to 1.25
- b_out: bfloat16 [768], replicated, may hold values from -3 to 3
- ln1_gain: bfloat16 [768], replicated, may hold values from 0.5 to 1.5
- ln1_bias: bfloat16 [768], replicated, may hold values from -2 to 2
- w_in: bfloat16 [768, 3072], replicated, may hold values from -0.21875 to 0.21875
- b_in: bfloat16 [3072], replicated, may hold values from -3 to 3
- w_down: bfloat16 [3072, 768], replicated, may hold values from -0.109375 to 0.109375
- b_down: bfloat16 [768], replicated, may hold values from -3 to 3
- ln2_gain: bfloat16 [768], replicated, may hold values from 0.5 to 1.5
- ln2_bias: bfloat16 [768], replicated, may hold values from -0.29882812 to 0.29882812
Outputs:
- losses: float32 [256], P(('twin', 'dp'))
- hidden_grad: bfloat16 [64, 512, 768], P(('twin', 'dp'))
- grad_w_qkv: float32 [768, 2304], P('dp')
- grad_b_query: float32 [768], P('dp')
- grad_b_value: float32 [768], P('dp')
- grad_w_out: float32 [768, 768], P('dp')
- grad_b_out: float32 [768], P('dp')
- grad_ln1_gain: float32 [768], P('dp')
- grad_ln1_bias: float32 [768], P('dp')
- grad_w_in: float32 [768, 3072], P('dp')
- grad_b_in: float32 [3072], P('dp')
- grad_w_down: float32 [3072, 768], P('dp')
- grad_b_down: float32 [768], P('dp')
- grad_ln2_gain: float32 [768], P('dp')
- grad_ln2_bias: float32 [768], P('dp')
Inputs may be any that keep to these rules, and one draw needn't show every extreme that they name: `segment_ids`: in each row the ids never fall; every id of 0 to 7 occurs, on 1 to 128 tokens. `targets`: every positive is the target of exactly one anchor.
All inputs are finite; a program needn't handle non-finite values.
Results may differ from a plain program's by a relative error of at most 0.012.
Values may be sent and summed in bfloat16 or wider, within the bound.
No kernel may reach another device: no remote copies, remote signals or barrier semaphores. Data moves between devices by JAX's collectives and lax.ppermute only.
A program may use at most 192 MiB of HBM per device.

v0:
```python
import jax
import jax.numpy as jnp
from jax import lax
from jax.sharding import PartitionSpec as P

D = 768
HEADS = 12
HEAD_DIM = 64
SEG = 8
cosine_scale = 64.0
loss_scale = 32.0
norm_epsilon = 1e-12
unit_epsilon = 1e-06
masked_score = -1e30


def layer_norm(inputs, norm_gain, norm_shift):
    middle = jnp.mean(inputs, axis=-1, keepdims=True)
    centered = inputs - middle
    spread = jnp.mean(centered * centered, axis=-1, keepdims=True)
    return centered * lax.rsqrt(spread + norm_epsilon) * norm_gain + norm_shift


def gelu_exact(inputs):
    return 0.5 * inputs * (1.0 + lax.erf(inputs * 0.5**0.5))


def contract_rows(left, right):
    return lax.dot_general(
        left, right, (((0,), (0,)), ((), ())), preferred_element_type=jnp.float32
    )


def contract_cols(left, right):
    return lax.dot_general(
        left, right, (((1,), (1,)), ((), ())), preferred_element_type=jnp.float32
    )


def split_heads(row_qkv):
    length = row_qkv.shape[0]
    query_heads = row_qkv[:, :D].reshape(length, HEADS, HEAD_DIM)
    key_heads = row_qkv[:, D : 2 * D].reshape(length, HEADS, HEAD_DIM)
    value_heads = row_qkv[:, 2 * D :].reshape(length, HEADS, HEAD_DIM)
    return (query_heads, key_heads, value_heads)


def masked_scores(query_heads, key_heads, row_seg):
    scores = jnp.einsum(
        "qhd,khd->hqk", query_heads, key_heads, preferred_element_type=jnp.float32
    ) * HEAD_DIM ** (-0.5)
    same_doc = (row_seg[:, None] == row_seg[None, :])[None]
    return (jnp.where(same_doc, scores, masked_score), same_doc)


def rank_loss(sims, wanted):
    row_top = jnp.max(sims, axis=1, keepdims=True)
    weights = jnp.exp(sims - row_top)
    row_total = jnp.sum(weights, axis=1, keepdims=True)
    column = lax.broadcasted_iota(jnp.int32, sims.shape, 1)
    target_hit = column == wanted[:, None]
    picked = jnp.sum(jnp.where(target_hit, sims, 0.0), axis=1)
    losses = row_top[:, 0] + jnp.log(row_total[:, 0]) - picked
    slope = (loss_scale * (weights / row_total - target_hit.astype(jnp.float32))).astype(
        jnp.bfloat16
    )
    return (losses, slope)


def body(
    hidden,
    segment_ids,
    targets,
    w_qkv,
    b_query,
    b_value,
    w_out,
    b_out,
    ln1_gain,
    ln1_bias,
    w_in,
    b_in,
    w_down,
    b_down,
    ln2_gain,
    ln2_bias,
):
    row_count, length, width = hidden.shape
    token_count = row_count * length
    tokens = hidden.reshape(token_count, width)
    bias_qkv = jnp.concatenate(
        [b_query.astype(jnp.float32), jnp.zeros((width,), jnp.float32), b_value.astype(jnp.float32)]
    )
    qkv_all = (jnp.dot(tokens, w_qkv, preferred_element_type=jnp.float32) + bias_qkv).astype(
        jnp.bfloat16
    )
    qkv_rows = qkv_all.reshape(row_count, length, 3 * width)

    def attend_forward(row_pack):
        row_qkv, row_seg = row_pack
        query_heads, key_heads, value_heads = split_heads(row_qkv)
        scores, same_doc = masked_scores(query_heads, key_heads, row_seg)
        row_top = jnp.max(scores, axis=-1, keepdims=True)
        weights = jnp.exp(scores - row_top)
        row_total = jnp.sum(weights, axis=-1, keepdims=True)
        prob_rows = (weights / row_total).astype(jnp.bfloat16)
        context = jnp.einsum(
            "hqk,khd->qhd", prob_rows, value_heads, preferred_element_type=jnp.float32
        )
        return (context.reshape(length, width).astype(jnp.bfloat16), row_top + jnp.log(row_total))

    context, log_total = lax.map(attend_forward, (qkv_rows, segment_ids))
    context_flat = context.reshape(token_count, width)
    attended = jnp.dot(context_flat, w_out, preferred_element_type=jnp.float32) + b_out.astype(
        jnp.float32
    )
    normed_one, norm_one_back = jax.vjp(
        layer_norm,
        tokens.astype(jnp.float32) + attended,
        ln1_gain.astype(jnp.float32),
        ln1_bias.astype(jnp.float32),
    )
    normed_low = normed_one.astype(jnp.bfloat16)
    hidden_pre = jnp.dot(normed_low, w_in, preferred_element_type=jnp.float32) + b_in.astype(
        jnp.float32
    )
    active, gelu_back = jax.vjp(gelu_exact, hidden_pre)
    active_low = active.astype(jnp.bfloat16)
    branch = jnp.dot(active_low, w_down, preferred_element_type=jnp.float32) + b_down.astype(
        jnp.float32
    )
    output, norm_two_back = jax.vjp(
        layer_norm, normed_one + branch, ln2_gain.astype(jnp.float32), ln2_bias.astype(jnp.float32)
    )
    member = (segment_ids[:, None, :] == jnp.arange(SEG, dtype=jnp.int32)[None, :, None]).astype(
        jnp.float32
    )
    counts = jnp.sum(member, axis=2, keepdims=True)

    def pool_units(out_rows):
        pooled = (
            jnp.einsum("rsl,rld->rsd", member, out_rows, precision=lax.Precision.HIGHEST) / counts
        )
        unit_rows = pooled * lax.rsqrt(
            jnp.mean(pooled * pooled, axis=-1, keepdims=True) + unit_epsilon
        )
        return unit_rows.reshape(row_count * SEG, width)

    unit_rows, pool_back = jax.vjp(pool_units, output.reshape(row_count, length, width))
    unit_low = unit_rows.astype(jnp.bfloat16)
    gathered = lax.all_gather(unit_low, ("twin", "dp"), axis=0, tiled=True)
    anchor_count = gathered.shape[0] // 2
    anchors = gathered[:anchor_count]
    positives = gathered[anchor_count:]
    factor = cosine_scale / width
    devices = lax.axis_size(("twin", "dp"))
    loss_share = anchor_count // devices
    loss_start = lax.axis_index(("twin", "dp")) * loss_share
    all_losses, slope = rank_loss(contract_cols(anchors, positives) * factor, targets)
    losses = lax.dynamic_slice_in_dim(all_losses, loss_start, loss_share, 0)
    sentences = unit_low.shape[0]
    offset = lax.axis_index("dp") * sentences
    anchor_rows = (
        jnp.dot(
            lax.dynamic_slice_in_dim(slope, offset, sentences, 0),
            positives,
            preferred_element_type=jnp.float32,
        )
        * factor
    )
    positive_rows = (
        contract_rows(lax.dynamic_slice_in_dim(slope, offset, sentences, 1), anchors) * factor
    )
    unit_grad = jnp.where(lax.axis_index("twin") == 0, anchor_rows, positive_rows)
    grad_output = pool_back(unit_grad)[0].reshape(token_count, width)
    grad_sum_two, grad_ln2_gain, grad_ln2_bias = norm_two_back(grad_output)
    grad_branch = grad_sum_two.astype(jnp.bfloat16)
    grad_w_down = contract_rows(active_low, grad_branch)
    grad_b_down = jnp.sum(grad_branch, axis=0, dtype=jnp.float32)
    grad_active = contract_cols(grad_branch, w_down)
    grad_pre = gelu_back(grad_active)[0].astype(jnp.bfloat16)
    grad_w_in = contract_rows(normed_low, grad_pre)
    grad_b_in = jnp.sum(grad_pre, axis=0, dtype=jnp.float32)
    grad_normed = contract_cols(grad_pre, w_in) + grad_sum_two
    grad_sum_one, grad_ln1_gain, grad_ln1_bias = norm_one_back(grad_normed)
    grad_attended = grad_sum_one.astype(jnp.bfloat16)
    grad_w_out = contract_rows(context_flat, grad_attended)
    grad_b_out = jnp.sum(grad_attended, axis=0, dtype=jnp.float32)
    grad_context = (
        contract_cols(grad_attended, w_out).astype(jnp.bfloat16).reshape(row_count, length, width)
    )

    def attend_backward(row_pack):
        row_qkv, row_seg, row_lse, row_grad = row_pack
        query_heads, key_heads, value_heads = split_heads(row_qkv)
        scores, same_doc = masked_scores(query_heads, key_heads, row_seg)
        prob_rows = jnp.where(same_doc, jnp.exp(scores - row_lse), 0.0)
        grad_heads = row_grad.reshape(length, HEADS, HEAD_DIM)
        grad_value = jnp.einsum(
            "hqk,qhd->khd",
            prob_rows.astype(jnp.bfloat16),
            grad_heads,
            preferred_element_type=jnp.float32,
        )
        grad_prob = jnp.einsum(
            "qhd,khd->hqk", grad_heads, value_heads, preferred_element_type=jnp.float32
        )
        inner = jnp.sum(prob_rows * grad_prob, axis=-1, keepdims=True)
        grad_scores = (prob_rows * (grad_prob - inner)).astype(jnp.bfloat16)
        grad_query = jnp.einsum(
            "hqk,khd->qhd", grad_scores, key_heads, preferred_element_type=jnp.float32
        ) * HEAD_DIM ** (-0.5)
        grad_key = jnp.einsum(
            "hqk,qhd->khd", grad_scores, query_heads, preferred_element_type=jnp.float32
        ) * HEAD_DIM ** (-0.5)
        return jnp.concatenate(
            [
                grad_query.reshape(length, width),
                grad_key.reshape(length, width),
                grad_value.reshape(length, width),
            ],
            axis=1,
        ).astype(jnp.bfloat16)

    grad_qkv = lax.map(attend_backward, (qkv_rows, segment_ids, log_total, grad_context))
    grad_qkv = grad_qkv.reshape(token_count, 3 * width)
    grad_w_qkv = contract_rows(tokens, grad_qkv)
    grad_b_query = jnp.sum(grad_qkv[:, :width], axis=0, dtype=jnp.float32)
    grad_b_value = jnp.sum(grad_qkv[:, 2 * width :], axis=0, dtype=jnp.float32)
    hidden_grad = (
        (contract_cols(grad_qkv, w_qkv) + grad_sum_one)
        .astype(jnp.bfloat16)
        .reshape(row_count, length, width)
    )
    (
        grad_w_qkv,
        grad_b_query,
        grad_b_value,
        grad_w_out,
        grad_b_out,
        grad_ln1_gain,
        grad_ln1_bias,
        grad_w_in,
        grad_b_in,
        grad_w_down,
        grad_b_down,
        grad_ln2_gain,
        grad_ln2_bias,
    ) = (
        lax.psum_scatter(grad_w_qkv, "dp", scatter_dimension=0, tiled=True),
        lax.psum_scatter(grad_b_query, "dp", scatter_dimension=0, tiled=True),
        lax.psum_scatter(grad_b_value, "dp", scatter_dimension=0, tiled=True),
        lax.psum_scatter(grad_w_out, "dp", scatter_dimension=0, tiled=True),
        lax.psum_scatter(grad_b_out, "dp", scatter_dimension=0, tiled=True),
        lax.psum_scatter(grad_ln1_gain, "dp", scatter_dimension=0, tiled=True),
        lax.psum_scatter(grad_ln1_bias, "dp", scatter_dimension=0, tiled=True),
        lax.psum_scatter(grad_w_in, "dp", scatter_dimension=0, tiled=True),
        lax.psum_scatter(grad_b_in, "dp", scatter_dimension=0, tiled=True),
        lax.psum_scatter(grad_w_down, "dp", scatter_dimension=0, tiled=True),
        lax.psum_scatter(grad_b_down, "dp", scatter_dimension=0, tiled=True),
        lax.psum_scatter(grad_ln2_gain, "dp", scatter_dimension=0, tiled=True),
        lax.psum_scatter(grad_ln2_bias, "dp", scatter_dimension=0, tiled=True),
    )
    (
        grad_w_qkv,
        grad_b_query,
        grad_b_value,
        grad_w_out,
        grad_b_out,
        grad_ln1_gain,
        grad_ln1_bias,
        grad_w_in,
        grad_b_in,
        grad_w_down,
        grad_b_down,
        grad_ln2_gain,
        grad_ln2_bias,
    ) = (
        lax.psum(grad_w_qkv.astype(jnp.bfloat16), "twin").astype(jnp.float32),
        lax.psum(grad_b_query.astype(jnp.bfloat16), "twin").astype(jnp.float32),
        lax.psum(grad_b_value.astype(jnp.bfloat16), "twin").astype(jnp.float32),
        lax.psum(grad_w_out.astype(jnp.bfloat16), "twin").astype(jnp.float32),
        lax.psum(grad_b_out.astype(jnp.bfloat16), "twin").astype(jnp.float32),
        lax.psum(grad_ln1_gain.astype(jnp.bfloat16), "twin").astype(jnp.float32),
        lax.psum(grad_ln1_bias.astype(jnp.bfloat16), "twin").astype(jnp.float32),
        lax.psum(grad_w_in.astype(jnp.bfloat16), "twin").astype(jnp.float32),
        lax.psum(grad_b_in.astype(jnp.bfloat16), "twin").astype(jnp.float32),
        lax.psum(grad_w_down.astype(jnp.bfloat16), "twin").astype(jnp.float32),
        lax.psum(grad_b_down.astype(jnp.bfloat16), "twin").astype(jnp.float32),
        lax.psum(grad_ln2_gain.astype(jnp.bfloat16), "twin").astype(jnp.float32),
        lax.psum(grad_ln2_bias.astype(jnp.bfloat16), "twin").astype(jnp.float32),
    )
    return (
        losses,
        hidden_grad,
        grad_w_qkv,
        grad_b_query,
        grad_b_value,
        grad_w_out,
        grad_b_out,
        grad_ln1_gain,
        grad_ln1_bias,
        grad_w_in,
        grad_b_in,
        grad_w_down,
        grad_b_down,
        grad_ln2_gain,
        grad_ln2_bias,
    )


def solution(mesh):
    placed = (
        P(("twin", "dp"), None, None),
        P(("twin", "dp"), None),
        P(),
        P(),
        P(),
        P(),
        P(),
        P(),
        P(),
        P(),
        P(),
        P(),
        P(),
        P(),
        P(),
        P(),
    )
    return jax.shard_map(
        body,
        mesh=mesh,
        in_specs=placed,
        out_specs=(
            P(("twin", "dp")),
            P(("twin", "dp"), None, None),
            P("dp", None),
            P("dp"),
            P("dp"),
            P("dp", None),
            P("dp"),
            P("dp"),
            P("dp"),
            P("dp", None),
            P("dp"),
            P("dp", None),
            P("dp"),
            P("dp"),
            P("dp"),
        ),
        check_vma=False,
    )
```

profile of v0, /device:TPU:0, one launch (start us, length us, event | category | flops | bytes accessed | tf_op | source)
XLA Modules:
  0.0 667.8 jit_solution(16013698214673223419)
XLA Ops:
  9.2 7.3 %add_convert_fusion.1 = bf16[1024,2304]{1,0:T(8,128)(2,1)} fusion(bf16[1024,768]{1,0:T(8,128)(2,1)} %bitcast.178, bf16[768,2304]{1,0:T(8,128)(2,1)S(1)} %copy-done, f32[2304]{0:T(1024)S(1)} %pad_maximum_fusion), kind=kOutput, calls=%fused_computation.35 | convolution fusion | flops 3628597248 | bytes 9839616 | tf_op jit(solution)/shard_map/dot_general | solution.py:94
  16.5 6.7 copy.53
  23.8 38.7 %while.22 = (s32[]{:T(128)}, bf16[2,512,768]{2,1,0:T(8,128)(2,1)}, f32[2,12,512,1]{2,1,3,0:T(8,128)}, bf16[2,512,2304]{1,2,0:T(8,128)(2,1)}, s32[2,512]{1,0:T(2,128)S(1)}, /*index=5*/s32[]{:T(128)}) while((s32[]{:T(128)}, bf16[2,512,768]{2,1,0:T(8,128)(2,1)}, f32[2,12,512,1]{2,1,3,0:T(8,128)}, bf16[2,512,2304]{1,2,0:T(8,128)(2,1)}, ...), condition=%wide.region_3.4_spmd, body=%wide.region_0.3_spmd.sunk | while | flops 843704320 | bytes 55786600 | solution.py:112
  67.9 9.4 %multiply_convert_fusion.3 = (bf16[1024,3072]{1,0:T(8,128)(2,1)S(1)}, f32[1024,3072]{1,0:T(8,128)}) fusion(f32[3072]{0:T(1024)S(1)} %convert_element_type.203, bf16[768,3072]{1,0:T(8,128)(2,1)S(1)} %bitcast.177, f32[1024,768]{1,0:T(8,128)S(1)} %get-tuple-element.228, f32[768]{0:T(1024)S(1)} %convert_element_type.201, f32[768]{0:T(1024)S(1)} %convert_element_type.200, ...), kind=kOutput, calls=%fused_computation.33 | convolution fusion | flops 4854644736 | bytes 26765312 | tf_op jit(solution)/shard_map/dot_general | solution.py:124
  86.6 45.3 %all_gather.3 = bf16[512,768]{1,0:T(8,128)(2,1)S(1)} all-gather(bf16[16,768]{1,0:T(8,128)(2,1)S(1)} %fusion.29), channel_id=1, replica_groups=mesh['twin'=2,'dp'=16] {'twin','dp'}, dimensions={0}, use_global_device_ids=true | all-gather | bytes 811008 | tf_op jit(solution)/shard_map/all_gather | solution.py:151
  145.8 15.0 %convert_reduce_fusion = (f32[3072]{0:T(1024)}, bf16[1024,3072]{1,0:T(8,128)(2,1)S(1)}) fusion(bf16[1024,768]{1,0:T(8,128)(2,1)S(1)} %get-tuple-element.210, bf16[3072,768]{1,0:T(8,128)(2,1)S(1)} %bitcast.175, f32[1024,3072]{1,0:T(8,128)} %get-tuple-element.230, f32[3072]{0:T(1024)S(1)} %copy-done.46), kind=kOutput, calls=%fused_computation.31 | convolution fusion | flops 4882166784 | bytes 25190400 | tf_op jit(solution)/shard_map/dot_general | solution.py:35
  160.8 11.3 %multiply_reduce_fusion.1 = (f32[768]{0:T(1024)}, f32[1024]{0:T(1024)S(1)}, f32[768]{0:T(1024)}, f32[1024,768]{1,0:T(8,128)S(1)}) fusion(f32[1024,768]{1,0:T(8,128)S(1)} %copy-done.9, f32[1024]{0:T(1024)S(1)} %fusion.36, f32[1024]{0:T(1024)S(1)} %broadcast_multiply_fusion.1, f32[768]{0:T(1024)S(1)} %convert_element_type.200, ...), kind=kOutput, calls=%fused_computation.43 | convolution fusion | flops 4839699456 | bytes 20472832 | tf_op jit(solution)/shard_map/dot_general | solution.py:35
  184.5 85.6 %while.23 = (s32[]{:T(128)}, bf16[2,512,2304]{1,2,0:T(8,128)(2,1)}, bf16[2,512,2304]{1,2,0:T(8,128)(2,1)}, s32[2,512]{1,0:T(2,128)S(1)}, f32[2,12,512,1]{2,1,3,0...) while((s32[]{:T(128)}, bf16[2,512,2304]{1,2,0:T(8,128)(2,1)}, bf16[2,512,2304]{1,2,0:T(8,128)(2,1)}, ...), condition=%wide.region_20.21_spmd, body=%wide.region_18.20_spmd.sunk | while | flops 2079188992 | bytes 181877680 | solution.py:225
  187.9 6.4 fusion.129
  199.2 11.5 %multiply_reduce_fusion.9 = (f32[12,512]{1,0:T(8,128)S(1)}, f32[12,512,512]{1,2,0:T(8,128)}) fusion(f32[12,512]{1,0:T(8,128)} %dynamic-slice_bitcast_fusion.7, f32[12,512,512]{1,2,0:T(8,128)} %fusion.129, pred[512,512]{0,1:T(8,128)(4,1)} %broadcast_compare_fusion.5, bf16[512,12,64]{0,2,1:T(8,128)(2,1)} %bitcast.162, bf16[512,12,64]{0,2,1:T(8,128)(2,1)} %bitcast.160), kind=kOutput, calls=%fused_computation.15.clone.1 | convolution fusion | flops 421521408 | bytes 27049984 | tf_op jit(solution)/shard_map/while/body/eval_jaxpr/qhd,khd->hqk/dot_general | solution.py:205
  212.6 7.1 %multiply_convert_fusion.9 = bf16[12,512,512]{1,2,0:T(8,128)(2,1)S(1)} fusion(f32[12,512,512]{1,2,0:T(8,128)} %get-tuple-element.330, f32[12,512]{1,0:T(8,128)S(1)} %get-tuple-element.331, f32[12,512]{1,0:T(8,128)S(1)} %copy-done.15, f32[12,512,512]{1,2,0:T(8,128)S(1)} %bitcast.150, pred[512,512]{0,1:T(8,128)(4,1)S(1)} %copy-done.10), kind=kLoop, calls=%fused_computation.14.clone.1 | loop fusion | flops 22020096 | bytes 31768576 | tf_op jit(solution)/shard_map/while/body/eval_jaxpr/convert_element_type | solution.py:209
  230.6 6.4 fusion.129
  241.8 11.5 %multiply_reduce_fusion.9 = (f32[12,512]{1,0:T(8,128)S(1)}, f32[12,512,512]{1,2,0:T(8,128)}) fusion(f32[12,512]{1,0:T(8,128)} %dynamic-slice_bitcast_fusion.7, f32[12,512,512]{1,2,0:T(8,128)} %fusion.129, pred[512,512]{0,1:T(8,128)(4,1)} %broadcast_compare_fusion.5, bf16[512,12,64]{0,2,1:T(8,128)(2,1)} %bitcast.162, bf16[512,12,64]{0,2,1:T(8,128)(2,1)} %bitcast.160), kind=kOutput, calls=%fused_computation.15.clone.1 | convolution fusion | flops 421521408 | bytes 27049984 | tf_op jit(solution)/shard_map/while/body/eval_jaxpr/qhd,khd->hqk/dot_general | solution.py:205
  254.9 7.1 %multiply_convert_fusion.9 = bf16[12,512,512]{1,2,0:T(8,128)(2,1)S(1)} fusion(f32[12,512,512]{1,2,0:T(8,128)} %get-tuple-element.330, f32[12,512]{1,0:T(8,128)S(1)} %get-tuple-element.331, f32[12,512]{1,0:T(8,128)S(1)} %copy-done.15, f32[12,512,512]{1,2,0:T(8,128)S(1)} %bitcast.150, pred[512,512]{0,1:T(8,128)(4,1)S(1)} %copy-done.10), kind=kLoop, calls=%fused_computation.14.clone.1 | loop fusion | flops 22020096 | bytes 31768576 | tf_op jit(solution)/shard_map/while/body/eval_jaxpr/convert_element_type | solution.py:209
  270.1 9.5 %convolution_bitcast_fusion = f32[768,2304]{0,1:T(8,128)} fusion(bf16[2,512,2304]{1,2,0:T(8,128)(2,1)} %get-tuple-element.77, bf16[2,512,768]{2,1,0:T(8,128)(2,1)} %param.20), kind=kOutput, calls=%fused_computation.36 | convolution fusion | flops 3623878656 | bytes 13369344 | tf_op jit(solution)/shard_map/dot_general | solution.py:29
  279.7 8.0 %copy.63 = f32[768,2304]{1,0:T(8,128)} copy(f32[768,2304]{0,1:T(8,128)} %convolution_bitcast_fusion) | data formatting | bytes 14155776
  288.4 11.4 %fusion.41 = f32[768,3072]{1,0:T(8,128)} fusion(bf16[1024,3072]{1,0:T(8,128)(2,1)} %copy-done.14, f32[1024,768]{1,0:T(8,128)} %copy-done.8, f32[768]{0:T(1024)S(1)} %copy-done.31, f32[768]{0:T(1024)S(1)} %copy-done.27, f32[1024]{0:T(1024)S(1)} %copy-done.24, f32[1024]{0:T(1024)S(1)} %copy-done.22), kind=kOutput, calls=%fused_computation.120 | convolution fusion | flops 4835770368 | bytes 18888704 | tf_op jit(solution)/shard_map/dot_general | solution.py:29
  299.9 10.2 %fusion.55 = f32[3072,768]{1,0:T(8,128)} fusion(bf16[1024,3072]{1,0:T(8,128)(2,1)} %copy-done.62, bf16[1024,768]{1,0:T(8,128)(2,1)} %copy-done.17), kind=kOutput, calls=%fused_computation.132 | convolution fusion | flops 4831838208 | bytes 17301504 | tf_op jit(solution)/shard_map/dot_general | solution.py:29
  310.3 7.0 %copy.57 = bf16[2,512,2304]{2,1,0:T(8,128)(2,1)} copy(bf16[2,512,2304]{1,2,0:T(8,128)(2,1)} %get-tuple-element.77) | data formatting | bytes 9437184 | tf_op jit(solution)/shard_map/while | solution.py:225
  322.1 61.6 %all-reduce.9 = (bf16[768]{0:T(1024)(128)(2,1)}, bf16[768]{0:T(1024)(128)(2,1)}, bf16[768]{0:T(1024)(128)(2,1)}, bf16[768]{0:T(1024)(128)(2,1)}, bf16[768]{0:T(1...) all-reduce(f32[768]{0:T(1024)} %get-tuple-element.161, ...), channel_id=3, replica_groups=mesh['twin'=2,'dp'=16] {'dp'}, use_global_device_ids=true, to_apply=%region_24.25.clone | all-reduce | flops 9216 | bytes 55296
  414.6 75.3 %reduce-scatter.9.cloned.1.call-done = f32[48,3072]{1,0:T(8,128)} async-done(((f32[768,3072]{1,0:T(8,128)}), f32[48,3072]{1,0:T(8,128)}) %reduce-scatter.9.cloned.1.call-update) | async-done | bytes 589840 | tf_op jit(solution)/shard_map/reduce_scatter | solution.py:257
  491.7 113.9 %reduce-scatter.11.cloned.1.call-done = f32[192,768]{1,0:T(8,128)} async-done(((f32[3072,768]{1,0:T(8,128)}), f32[192,768]{1,0:T(8,128)}) %reduce-scatter.11.cloned.1.call-update) | async-done | bytes 589840 | tf_op jit(solution)/shard_map/reduce_scatter | solution.py:259
  607.4 7.8 %add_convert_fusion.2 = bf16[1024,768]{1,0:T(8,128)(2,1)} fusion(f32[1024,768]{1,0:T(8,128)} %copy-done.12, bf16[1024,2304]{1,0:T(8,128)(2,1)} %bitcast.166, bf16[768,2304]{1,0:T(8,128)(2,1)S(1)} %copy-done, f32[1024]{0:T(1024)S(1)} %copy-done.41), kind=kOutput, calls=%fused_computation.47 | convolution fusion | flops 3626237952 | bytes 12980224 | tf_op jit(solution)/shard_map/dot_general | solution.py:35
  615.1 38.7 %all-reduce.14.cloned.1.call-done = (bf16[48,2304]{0,1:T(8,128)(2,1)}, bf16[48,768]{1,0:T(8,128)(2,1)}, bf16[48,3072]{1,0:T(8,128)(2,1)}, bf16[192,768]{1,0:T(8,128)(2,1)}) async-done(((bf16[48,2304]{0,1:T(8,128)(2,1)}, bf16[48,768]{1,0:T(8,128)(2,1)}, bf16[48,3072]{1,0:T(8,128)(2,1)}, bf16[192,768]{1,0:T(8,128)(2,1)}), (bf16[48,2304]{0,1:T(8,128)(2,1)}, bf16[48,768]{1,0:T(8,128)(2,1)}, ...) | async-done | bytes 884752 | tf_op jit(solution)/shard_map/psum | solution.py:279
  (305 shorter events, 162.5 us)
Async XLA Ops:
  7.2 403.8 %reduce-scatter.7.cloned.1.call-start = ((), (), s32[]{:S(2)}) async-start(), calls=%async_computation.4 | async-start | bytes 2506752 | tf_op jit(solution)/shard_map/reduce_scatter | solution.py:253
  23.8 38.7 %copy-start.54 = (bf16[768]{0:T(1024)(128)(2,1)S(1)}, bf16[768]{0:T(1024)(128)(2,1)}, u32[]{:S(2)}) copy-start(bf16[768]{0:T(1024)(128)(2,1)} %param.27) | copy-start | bytes 4612
  66.6 105.5 %copy-start.21 = (f32[1024]{0:T(1024)}, f32[1024]{0:T(1024)S(1)}, u32[]{:S(2)}) copy-start(f32[1024]{0:T(1024)S(1)} %broadcast_multiply_fusion.1) | copy-start | bytes 12292
  67.7 104.4 %copy-start.23 = (f32[1024]{0:T(1024)}, f32[1024]{0:T(1024)S(1)}, u32[]{:S(2)}) copy-start(f32[1024]{0:T(1024)S(1)} %fusion.36) | copy-start | bytes 12292
  67.7 104.4 %copy-start.26 = (f32[768]{0:T(1024)}, f32[768]{0:T(1024)S(1)}, u32[]{:S(2)}) copy-start(f32[768]{0:T(1024)S(1)} %convert_element_type.200) | copy-start | bytes 9220
  84.7 48.5 %copy-start.53 = (s32[256]{0:T(256)S(1)}, s32[256]{0:T(256)}, u32[]{:S(2)}) copy-start(s32[256]{0:T(256)} %param.22) | copy-start | bytes 3076
  86.0 47.1 %copy-start.19 = (f32[2,8,768]{2,1,0:T(8,128)}, f32[2,8,768]{2,1,0:T(8,128)S(1)}, u32[]{:S(2)}) copy-start(f32[2,8,768]{2,1,0:T(8,128)S(1)} %get-tuple-element.234) | copy-start | bytes 147460
  86.0 47.2 %copy-start.51 = (f32[2,8]{1,0:T(2,128)}, f32[2,8]{1,0:T(2,128)S(1)}, u32[]{:S(2)}) copy-start(f32[2,8]{1,0:T(2,128)S(1)} %get-tuple-element.233) | copy-start | bytes 196
  145.7 15.1 %copy-start.17 = (bf16[1024,768]{1,0:T(8,128)(2,1)}, bf16[1024,768]{1,0:T(8,128)(2,1)S(1)}, u32[]{:S(2)}) copy-start(bf16[1024,768]{1,0:T(8,128)(2,1)S(1)} %get-tuple-element.210) | copy-start | bytes 4718596
  145.8 15.0 %copy-start.9 = (f32[1024,768]{1,0:T(8,128)S(1)}, f32[1024,768]{1,0:T(8,128)}, u32[]{:S(2)}) copy-start(f32[1024,768]{1,0:T(8,128)} %copy-done.8) | copy-start | bytes 9437188
  180.2 232.4 %reduce-scatter.13.cloned.1.call-start = ((), (), s32[]{:S(2)}) async-start(), calls=%async_computation.7 | async-start | bytes 7520256
  199.2 11.6 %slice-start = ((s8[12582912]{0:T(1024)(128)(4,1)}), s8[4194304]{0:T(1024)(128)(4,1)S(1)}, s32[]{:S(2)}) async-start(s8[12582912]{0:T(1024)(128)(4,1)} %bitcast.149), calls=%async_computation.9 | async-start | bytes 8388608 | tf_op jit(solution)/shard_map/while
  199.2 11.6 %slice-start.1 = ((s8[12582912]{0:T(1024)(128)(4,1)}), s8[4194304]{0:T(1024)(128)(4,1)S(1)}, s32[]{:S(2)}) async-start(s8[12582912]{0:T(1024)(128)(4,1)} %bitcast.149), calls=%async_computation.10 | async-start | bytes 8388608 | tf_op jit(solution)/shard_map/while
  199.2 13.4 %slice-start.2 = ((s8[12582912]{0:T(1024)(128)(4,1)}), s8[4194304]{0:T(1024)(128)(4,1)S(1)}, s32[]{:S(2)}) async-start(s8[12582912]{0:T(1024)(128)(4,1)} %bitcast.149), calls=%async_computation.11 | async-start | bytes 8388608 | tf_op jit(solution)/shard_map/while
  199.2 13.4 %copy-start.10 = (pred[512,512]{0,1:T(8,128)(4,1)S(1)}, pred[512,512]{0,1:T(8,128)(4,1)}, u32[]{:S(2)}) copy-start(pred[512,512]{0,1:T(8,128)(4,1)} %broadcast_compare_fusion.5) | copy-start | bytes 786436 | tf_op jit(solution)/shard_map/while
  199.2 13.4 %copy-start.15 = (f32[12,512]{1,0:T(8,128)S(1)}, f32[12,512]{1,0:T(8,128)}, u32[]{:S(2)}) copy-start(f32[12,512]{1,0:T(8,128)} %dynamic-slice_bitcast_fusion.7) | copy-start | bytes 73732 | tf_op jit(solution)/shard_map/while
  241.8 11.5 %slice-start.1 = ((s8[12582912]{0:T(1024)(128)(4,1)}), s8[4194304]{0:T(1024)(128)(4,1)S(1)}, s32[]{:S(2)}) async-start(s8[12582912]{0:T(1024)(128)(4,1)} %bitcast.149), calls=%async_computation.10 | async-start | bytes 8388608 | tf_op jit(solution)/shard_map/while
  241.8 13.2 %slice-start.2 = ((s8[12582912]{0:T(1024)(128)(4,1)}), s8[4194304]{0:T(1024)(128)(4,1)S(1)}, s32[]{:S(2)}) async-start(s8[12582912]{0:T(1024)(128)(4,1)} %bitcast.149), calls=%async_computation.11 | async-start | bytes 8388608 | tf_op jit(solution)/shard_map/while
  241.8 13.2 %copy-start.10 = (pred[512,512]{0,1:T(8,128)(4,1)S(1)}, pred[512,512]{0,1:T(8,128)(4,1)}, u32[]{:S(2)}) copy-start(pred[512,512]{0,1:T(8,128)(4,1)} %broadcast_compare_fusion.5) | copy-start | bytes 786436 | tf_op jit(solution)/shard_map/while
  241.8 13.2 %copy-start.15 = (f32[12,512]{1,0:T(8,128)S(1)}, f32[12,512]{1,0:T(8,128)}, u32[]{:S(2)}) copy-start(f32[12,512]{1,0:T(8,128)} %dynamic-slice_bitcast_fusion.7) | copy-start | bytes 73732 | tf_op jit(solution)/shard_map/while
  287.7 202.1 %reduce-scatter.9.cloned.1.call-start = ((), (), s32[]{:S(2)}) async-start(), calls=%async_computation.5 | async-start | bytes 10027008 | tf_op jit(solution)/shard_map/reduce_scatter | solution.py:257
  299.9 305.6 %reduce-scatter.11.cloned.1.call-start = ((), (), s32[]{:S(2)}) async-start(), calls=%async_computation.6 | async-start | bytes 10027008 | tf_op jit(solution)/shard_map/reduce_scatter | solution.py:259
  310.2 343.6 %all-reduce.14.cloned.1.call-start = ((), (), s32[]{:S(2)}) async-start(), calls=%async_computation.8 | async-start | bytes 2506752 | tf_op jit(solution)/shard_map/psum | solution.py:279
  319.1 288.3 %copy-start.41 = (f32[1024]{0:T(1024)S(1)}, f32[1024]{0:T(1024)}, u32[]{:S(2)}) copy-start(f32[1024]{0:T(1024)} %copy-done.40) | copy-start | bytes 12292
  (66 other events, 273.1 us)
Sparse Core Ops, SparseCore 0:
  180.3 59.4 reduce-scatter.6
  287.8 86.7 reduce-scatter.12
  378.8 111.0 reduce-scatter.8
  494.4 111.1 reduce-scatter.10
  609.0 44.7 all-reduce.13
where the time goes:
time: 678 us; the launch traced here: 668 us
  waiting for transfers between devices  228 us (34%)
  matrix products  170 us (25%)
  blocking collectives  113 us (17%)
  local copies, waits for them, and re-layouts  75.6 us (11%)
  other arithmetic  65.3 us (10%)
  between operations  15.9 us (2%)
    reduce_scatter x1, waiting for transfers between devices, body(): lax.psum_scatter(grad_w_down, 'dp', scatter_dimension=0, tiled=True)  114 us
    reduce_scatter x1, waiting for transfers between devices, body(): lax.psum_scatter(grad_w_in, 'dp', scatter_dimension=0, tiled=True)  75.3 us
    unnamed x1, blocking collectives  61.6 us
    all_gather x1, blocking collectives, body(): gathered = lax.all_gather(unit_low, ('twin', 'dp'), axis=0, tiled=True)  45.3 us
    psum x1, waiting for transfers between devices, body(): lax.psum(grad_w_qkv.astype(jnp.bfloat16), 'twin').astype(jnp.float32)  38.7 us
    dot_general x5, matrix products, contract_cols(): lax.dot_general(left, right, (((1,), (1,)), ((), ())), preferred_element_...  38.7 us
    dot_general x5, matrix products, contract_rows(): lax.dot_general(left, right, (((0,), (0,)), ((), ())), preferred_element_...  35.4 us
    unnamed x131, local copies, waits for them, and re-layouts  29.5 us
  transfers between devices with their start and end apart: 5, of which 3 were waited for; matrix products, arithmetic and copies ran while one was open for 25% of the time, Pallas kernels for 0%

commit v1 on v0

--- a/solution.py
+++ b/solution.py
@@ -276,7 +276,9 @@
         grad_ln2_gain,
         grad_ln2_bias,
     ) = (
-        lax.psum(grad_w_qkv.astype(jnp.bfloat16), "twin").astype(jnp.float32),
+        jnp.sum(lax.all_gather(grad_w_qkv.astype(jnp.bfloat16), "twin"), axis=0).astype(
+            jnp.float32
+        ),
         lax.psum(grad_b_query.astype(jnp.bfloat16), "twin").astype(jnp.float32),
         lax.psum(grad_b_value.astype(jnp.bfloat16), "twin").astype(jnp.float32),
         lax.psum(grad_w_out.astype(jnp.bfloat16), "twin").astype(jnp.float32),

time: 678 us -> 625 us (0.922)
  waiting for transfers between devices: 228 us -> 162 us
  blocking collectives: 113 us -> 124 us
    reduce_scatter x1, waiting for transfers between devices: 75.3 us -> 35.6 us  [body(): lax.psum_scatter(grad_w_in, 'dp', scatter_dimension=0, tiled=True)]
    psum x1, waiting for transfers between devices: 38.7 us -> 13.1 us  [body(): lax.psum(grad_w_out.astype(jnp.bfloat16), 'twin').astype(jnp.float32)]
    all_gather x0 -> x1, blocking collectives: none -> 10.6 us  [body(): lax.all_gather(grad_w_qkv.astype(jnp.bfloat16), 'twin')]
    unnamed x131 -> x115, local copies, waits for them, and re-layouts: 29.5 us -> 24.4 us
  transfers between devices with their start and end apart: 5 -> 5, of which waited for: 3 -> 3; matrix products, arithmetic and copies ran while one was open for 25% -> 29% of each run, Pallas kernels for 0% -> 0%
where the time goes in v1:
time: 625 us; the launch traced here: 615 us
  matrix products  171 us (27%)
  waiting for transfers between devices  162 us (26%)
  blocking collectives  124 us (20%)
  local copies, waits for them, and re-layouts  70.1 us (11%)
  other arithmetic  70.1 us (11%)
  between operations  16 us (3%)
    reduce_scatter x1, waiting for transfers between devices, body(): lax.psum_scatter(grad_w_down, 'dp', scatter_dimension=0, tiled=True)  113 us
    unnamed x1, blocking collectives  62.8 us
    all_gather x1, blocking collectives, body(): gathered = lax.all_gather(unit_low, ('twin', 'dp'), axis=0, tiled=True)  45.3 us
    dot_general x5, matrix products, contract_cols(): lax.dot_general(left, right, (((1,), (1,)), ((), ())), preferred_element_...  38.7 us
    reduce_scatter x1, waiting for transfers between devices, body(): lax.psum_scatter(grad_w_in, 'dp', scatter_dimension=0, tiled=True)  35.6 us
    dot_general x5, matrix products, contract_rows(): lax.dot_general(left, right, (((0,), (0,)), ((), ())), preferred_element_...  35.3 us
    unnamed x115, local copies, waits for them, and re-layouts  24.4 us
    dot_general x2, matrix products, attend_backward(): jnp.einsum('qhd,khd->hqk', grad_heads, value_heads, preferred_element_typ...  23.6 us
  transfers between devices with their start and end apart: 5, of which 3 were waited for; matrix products, arithmetic and copies ran while one was open for 29% of the time, Pallas kernels for 0%

profile of v1, /device:TPU:0, one launch (start us, length us, event | category | flops | bytes accessed | tf_op | source)
XLA Modules:
  0.0 614.7 jit_solution(11413668231943065171)
XLA Ops:
  9.2 7.3 %add_convert_fusion.1 = bf16[1024,2304]{1,0:T(8,128)(2,1)} fusion(bf16[1024,768]{1,0:T(8,128)(2,1)} %bitcast.180, bf16[768,2304]{1,0:T(8,128)(2,1)S(1)} %copy-done, f32[2304]{0:T(1024)S(1)} %pad_maximum_fusion), kind=kOutput, calls=%fused_computation.35 | convolution fusion | flops 3628597248 | bytes 9839616 | tf_op jit(solution)/shard_map/dot_general | solution.py:94
  16.5 6.7 %copy.62 = bf16[2,512,2304]{1,2,0:T(8,128)(2,1)} copy(bf16[2,512,2304]{2,1,0:T(8,128)(2,1)} %bitcast.170) | data formatting | bytes 9437184 | tf_op jit(solution)/shard_map/while | solution.py:112
  23.8 38.7 %while.22 = (s32[]{:T(128)}, bf16[2,512,768]{2,1,0:T(8,128)(2,1)}, f32[2,12,512,1]{2,1,3,0:T(8,128)}, bf16[2,512,2304]{1,2,0:T(8,128)(2,1)}, s32[2,512]{1,0:T(2,128)S(1)}, /*index=5*/s32[]{:T(128)}) while((s32[]{:T(128)}, bf16[2,512,768]{2,1,0:T(8,128)(2,1)}, f32[2,12,512,1]{2,1,3,0:T(8,128)}, bf16[2,512,2304]{1,2,0:T(8,128)(2,1)}, ...), condition=%wide.region_3.4_spmd, body=%wide.region_0.3_spmd.sunk | while | flops 843704320 | bytes 55786600 | solution.py:112
  67.7 9.4 %multiply_convert_fusion.3 = (bf16[1024,3072]{1,0:T(8,128)(2,1)S(1)}, f32[1024,3072]{1,0:T(8,128)}) fusion(f32[3072]{0:T(1024)S(1)} %convert_element_type.205, bf16[768,3072]{1,0:T(8,128)(2,1)S(1)} %bitcast.179, f32[1024,768]{1,0:T(8,128)S(1)} %get-tuple-element.193, f32[768]{0:T(1024)S(1)} %convert_element_type.203, f32[768]{0:T(1024)S(1)} %convert_element_type.202, ...), kind=kOutput, calls=%fused_computation.33 | convolution fusion | flops 4854644736 | bytes 26765312 | tf_op jit(solution)/shard_map/dot_general | solution.py:124
  86.5 45.3 %all_gather.9 = bf16[512,768]{1,0:T(8,128)(2,1)S(1)} all-gather(bf16[16,768]{1,0:T(8,128)(2,1)S(1)} %fusion.29), channel_id=1, replica_groups=mesh['twin'=2,'dp'=16] {'twin','dp'}, dimensions={0}, use_global_device_ids=true | all-gather | bytes 811008 | tf_op jit(solution)/shard_map/all_gather | solution.py:151
  145.7 15.0 %convert_reduce_fusion = (f32[3072]{0:T(1024)}, bf16[1024,3072]{1,0:T(8,128)(2,1)S(1)}) fusion(bf16[1024,768]{1,0:T(8,128)(2,1)S(1)} %get-tuple-element.175, bf16[3072,768]{1,0:T(8,128)(2,1)S(1)} %bitcast.177, f32[1024,3072]{1,0:T(8,128)} %get-tuple-element.195, f32[3072]{0:T(1024)S(1)} %copy-done.39), kind=kOutput, calls=%fused_computation.31 | convolution fusion | flops 4882166784 | bytes 25190400 | tf_op jit(solution)/shard_map/dot_general | solution.py:35
  160.8 11.3 %multiply_reduce_fusion.1 = (f32[768]{0:T(1024)}, f32[1024]{0:T(1024)S(1)}, f32[768]{0:T(1024)}, f32[1024,768]{1,0:T(8,128)S(1)}) fusion(f32[1024,768]{1,0:T(8,128)S(1)} %copy-done.9, f32[1024]{0:T(1024)S(1)} %fusion.36, f32[1024]{0:T(1024)S(1)} %broadcast_multiply_fusion.1, f32[768]{0:T(1024)S(1)} %convert_element_type.202, ...), kind=kOutput, calls=%fused_computation.43 | convolution fusion | flops 4839699456 | bytes 20472832 | tf_op jit(solution)/shard_map/dot_general | solution.py:35
  180.2 11.5 %fusion.41 = f32[768,3072]{1,0:T(8,128)} fusion(bf16[1024,3072]{1,0:T(8,128)(2,1)} %copy-done.14, f32[1024,768]{1,0:T(8,128)} %copy-done.8, f32[768]{0:T(1024)} %copy-done.24, f32[768]{0:T(1024)S(1)} %convert_element_type.202, f32[1024]{0:T(1024)S(1)} %fusion.36, f32[1024]{0:T(1024)S(1)} %broadcast_multiply_fusion.1), kind=kOutput, calls=%fused_computation.120 | convolution fusion | flops 4835770368 | bytes 18888704 | tf_op jit(solution)/shard_map/dot_general | solution.py:29
  191.8 10.0 %fusion.55 = f32[3072,768]{1,0:T(8,128)} fusion(bf16[1024,3072]{1,0:T(8,128)(2,1)} %copy-done.55, bf16[1024,768]{1,0:T(8,128)(2,1)} %copy-done.17), kind=kOutput, calls=%fused_computation.132 | convolution fusion | flops 4831838208 | bytes 17301504 | tf_op jit(solution)/shard_map/dot_general | solution.py:29
  206.2 86.9 %while.23 = (s32[]{:T(128)}, bf16[2,512,2304]{1,2,0:T(8,128)(2,1)}, bf16[2,512,2304]{1,2,0:T(8,128)(2,1)}, s32[2,512]{1,0:T(2,128)S(1)}, f32[2,12,512,1]{2,1,3,0...) while((s32[]{:T(128)}, bf16[2,512,2304]{1,2,0:T(8,128)(2,1)}, bf16[2,512,2304]{1,2,0:T(8,128)(2,1)}, ...), condition=%wide.region_20.21_spmd, body=%wide.region_18.20_spmd.sunk | while | flops 2079188992 | bytes 181877680 | solution.py:225
  220.5 11.6 %multiply_reduce_fusion.9 = (f32[12,512]{1,0:T(8,128)S(1)}, f32[12,512,512]{1,2,0:T(8,128)}) fusion(f32[12,512]{1,0:T(8,128)} %dynamic-slice_bitcast_fusion.7, f32[12,512,512]{1,2,0:T(8,128)} %fusion.129, pred[512,512]{0,1:T(8,128)(4,1)} %broadcast_compare_fusion.5, bf16[512,12,64]{0,2,1:T(8,128)(2,1)} %bitcast.163, bf16[512,12,64]{0,2,1:T(8,128)(2,1)} %bitcast.161), kind=kOutput, calls=%fused_computation.15.clone.1 | convolution fusion | flops 421521408 | bytes 27049984 | tf_op jit(solution)/shard_map/while/body/eval_jaxpr/qhd,khd->hqk/dot_general | solution.py:205
  233.7 7.1 %multiply_convert_fusion.9 = bf16[12,512,512]{1,2,0:T(8,128)(2,1)S(1)} fusion(f32[12,512,512]{1,2,0:T(8,128)} %get-tuple-element.295, f32[12,512]{1,0:T(8,128)S(1)} %get-tuple-element.296, f32[12,512]{1,0:T(8,128)S(1)} %copy-done.15, f32[12,512,512]{1,2,0:T(8,128)S(1)} %bitcast.151, pred[512,512]{0,1:T(8,128)(4,1)S(1)} %copy-done.10), kind=kLoop, calls=%fused_computation.14.clone.1 | loop fusion | flops 22020096 | bytes 31768576 | tf_op jit(solution)/shard_map/while/body/eval_jaxpr/convert_element_type | solution.py:209
  251.6 7.5 %fusion.129 = f32[12,512,512]{1,2,0:T(8,128)} fusion(bf16[512,12,64]{0,2,1:T(8,128)(2,1)S(1)} %bitcast.154, bf16[512,12,64]{0,2,1:T(8,128)(2,1)S(1)} %bitcast.152), kind=kOutput, calls=%fused_computation.130.clone.1 | convolution fusion | flops 402653184 | bytes 14155776 | tf_op jit(solution)/shard_map/while/body/eval_jaxpr/qhd,khd->hqk/dot_general | solution.py:49
  264.1 12.1 %multiply_reduce_fusion.9 = (f32[12,512]{1,0:T(8,128)S(1)}, f32[12,512,512]{1,2,0:T(8,128)}) fusion(f32[12,512]{1,0:T(8,128)} %dynamic-slice_bitcast_fusion.7, f32[12,512,512]{1,2,0:T(8,128)} %fusion.129, pred[512,512]{0,1:T(8,128)(4,1)} %broadcast_compare_fusion.5, bf16[512,12,64]{0,2,1:T(8,128)(2,1)} %bitcast.163, bf16[512,12,64]{0,2,1:T(8,128)(2,1)} %bitcast.161), kind=kOutput, calls=%fused_computation.15.clone.1 | convolution fusion | flops 421521408 | bytes 27049984 | tf_op jit(solution)/shard_map/while/body/eval_jaxpr/qhd,khd->hqk/dot_general | solution.py:205
  277.9 7.1 %multiply_convert_fusion.9 = bf16[12,512,512]{1,2,0:T(8,128)(2,1)S(1)} fusion(f32[12,512,512]{1,2,0:T(8,128)} %get-tuple-element.295, f32[12,512]{1,0:T(8,128)S(1)} %get-tuple-element.296, f32[12,512]{1,0:T(8,128)S(1)} %copy-done.15, f32[12,512,512]{1,2,0:T(8,128)S(1)} %bitcast.151, pred[512,512]{0,1:T(8,128)(4,1)S(1)} %copy-done.10), kind=kLoop, calls=%fused_computation.14.clone.1 | loop fusion | flops 22020096 | bytes 31768576 | tf_op jit(solution)/shard_map/while/body/eval_jaxpr/convert_element_type | solution.py:209
  293.1 9.6 %convolution_bitcast_fusion = f32[768,2304]{0,1:T(8,128)} fusion(bf16[2,512,2304]{1,2,0:T(8,128)(2,1)} %get-tuple-element.77, bf16[2,512,768]{2,1,0:T(8,128)(2,1)} %param.20), kind=kOutput, calls=%fused_computation.36 | convolution fusion | flops 3623878656 | bytes 13369344 | tf_op jit(solution)/shard_map/dot_general | solution.py:29
  302.7 8.0 %copy.72 = f32[768,2304]{1,0:T(8,128)} copy(f32[768,2304]{0,1:T(8,128)} %convolution_bitcast_fusion) | data formatting | bytes 14155776
  310.8 6.8 %copy.66 = bf16[2,512,2304]{2,1,0:T(8,128)(2,1)} copy(bf16[2,512,2304]{1,2,0:T(8,128)(2,1)} %get-tuple-element.77) | data formatting | bytes 9437184 | tf_op jit(solution)/shard_map/while | solution.py:225
  319.2 35.6 %reduce-scatter.9.cloned.1.call-done = f32[48,3072]{1,0:T(8,128)} async-done(((f32[768,3072]{1,0:T(8,128)}), f32[48,3072]{1,0:T(8,128)}) %reduce-scatter.9.cloned.1.call-update) | async-done | bytes 589840 | tf_op jit(solution)/shard_map/reduce_scatter | solution.py:257
  356.6 113.4 %reduce-scatter.11.cloned.1.call-done = f32[192,768]{1,0:T(8,128)} async-done(((f32[3072,768]{1,0:T(8,128)}), f32[192,768]{1,0:T(8,128)}) %reduce-scatter.11.cloned.1.call-update) | async-done | bytes 589840 | tf_op jit(solution)/shard_map/reduce_scatter | solution.py:259
  471.9 7.8 %add_convert_fusion.2 = bf16[1024,768]{1,0:T(8,128)(2,1)} fusion(f32[1024,768]{1,0:T(8,128)} %copy-done.12, bf16[1024,2304]{1,0:T(8,128)(2,1)} %bitcast.166, bf16[768,2304]{1,0:T(8,128)(2,1)S(1)} %copy-done, f32[1024]{0:T(1024)S(1)} %copy-done.34), kind=kOutput, calls=%fused_computation.47 | convolution fusion | flops 3626237952 | bytes 12980224 | tf_op jit(solution)/shard_map/dot_general | solution.py:35
  484.9 62.8 %all-reduce.9 = (bf16[768]{0:T(1024)(128)(2,1)}, bf16[768]{0:T(1024)(128)(2,1)}, bf16[768]{0:T(1024)(128)(2,1)}, bf16[768]{0:T(1024)(128)(2,1)}, bf16[768]{0:T(1...) all-reduce(f32[768]{0:T(1024)} %get-tuple-element.127, ...), channel_id=4, replica_groups=mesh['twin'=2,'dp'=16] {'dp'}, use_global_device_ids=true, to_apply=%region_24.25.clone | all-reduce | flops 9216 | bytes 55296
  575.5 10.6 %all-gather = bf16[96,2304]{1,0:T(8,128)(2,1)} all-gather(bf16[48,2304]{1,0:T(8,128)(2,1)S(1)} %convert_element_type.220), channel_id=2, replica_groups=mesh['twin'=2,'dp'=16] {'twin'}, dimensions={0}, use_global_device_ids=true | all-gather | bytes 663552 | tf_op jit(solution)/shard_map/all_gather | solution.py:279
  589.6 13.1 %all-reduce.14.cloned.1.call-done = (bf16[48,768]{1,0:T(8,128)(2,1)}, bf16[48,3072]{1,0:T(8,128)(2,1)}, bf16[192,768]{1,0:T(8,128)(2,1)}) async-done(((bf16[48,768]{1,0:T(8,128)(2,1)}, bf16[48,3072]{1,0:T(8,128)(2,1)}, bf16[192,768]{1,0:T(8,128)(2,1)}), (bf16[48,768]{1,0:T(8,128)(2,1)}, bf16[48,3072]{1,0:T(8,128)(2,1)}, bf16[192,768]{1,0:T(8,128)(2,1)})) %all-reduce.14.cloned.1.call-update) | async-done | bytes 663568 | tf_op jit(solution)/shard_map/psum | solution.py:284
  (293 shorter events, 168.5 us)
Async XLA Ops:
  7.2 310.4 %reduce-scatter.7.cloned.1.call-start = ((), (), s32[]{:S(2)}) async-start(), calls=%async_computation.4 | async-start | bytes 2506752 | tf_op jit(solution)/shard_map/reduce_scatter | solution.py:253
  23.8 38.7 %copy-start.47 = (bf16[768]{0:T(1024)(128)(2,1)S(1)}, bf16[768]{0:T(1024)(128)(2,1)}, u32[]{:S(2)}) copy-start(bf16[768]{0:T(1024)(128)(2,1)} %param.27) | copy-start | bytes 4612
  84.5 48.5 %copy-start.46 = (s32[256]{0:T(256)S(1)}, s32[256]{0:T(256)}, u32[]{:S(2)}) copy-start(s32[256]{0:T(256)} %param.22) | copy-start | bytes 3076
  85.9 47.2 %copy-start.19 = (f32[2,8,768]{2,1,0:T(8,128)}, f32[2,8,768]{2,1,0:T(8,128)S(1)}, u32[]{:S(2)}) copy-start(f32[2,8,768]{2,1,0:T(8,128)S(1)} %get-tuple-element.199) | copy-start | bytes 147460
  85.9 47.2 %copy-start.44 = (f32[2,8]{1,0:T(2,128)}, f32[2,8]{1,0:T(2,128)S(1)}, u32[]{:S(2)}) copy-start(f32[2,8]{1,0:T(2,128)S(1)} %get-tuple-element.198) | copy-start | bytes 196
  145.7 15.0 %copy-start.17 = (bf16[1024,768]{1,0:T(8,128)(2,1)}, bf16[1024,768]{1,0:T(8,128)(2,1)S(1)}, u32[]{:S(2)}) copy-start(bf16[1024,768]{1,0:T(8,128)(2,1)S(1)} %get-tuple-element.175) | copy-start | bytes 4718596
  145.7 15.0 %copy-start.9 = (f32[1024,768]{1,0:T(8,128)S(1)}, f32[1024,768]{1,0:T(8,128)}, u32[]{:S(2)}) copy-start(f32[1024,768]{1,0:T(8,128)} %copy-done.8) | copy-start | bytes 9437188
  160.8 11.3 %copy-start.14 = (bf16[1024,3072]{1,0:T(8,128)(2,1)}, bf16[1024,3072]{1,0:T(8,128)(2,1)S(1)}, u32[]{:S(2)}) copy-start(bf16[1024,3072]{1,0:T(8,128)(2,1)S(1)} %get-tuple-element.206) | copy-start | bytes 18874372
  160.8 11.3 %copy-start.30 = (f32[1024]{0:T(1024)S(1)}, f32[1024]{0:T(1024)}, u32[]{:S(2)}) copy-start(f32[1024]{0:T(1024)} %copy-done.29) | copy-start | bytes 12292
  180.2 174.6 %reduce-scatter.9.cloned.1.call-start = ((), (), s32[]{:S(2)}) async-start(), calls=%async_computation.5 | async-start | bytes 10027008 | tf_op jit(solution)/shard_map/reduce_scatter | solution.py:257
  191.8 278.3 %reduce-scatter.11.cloned.1.call-start = ((), (), s32[]{:S(2)}) async-start(), calls=%async_computation.6 | async-start | bytes 10027008 | tf_op jit(solution)/shard_map/reduce_scatter | solution.py:259
  201.8 372.6 %reduce-scatter.13.cloned.1.call-start = ((), (), s32[]{:S(2)}) async-start(), calls=%async_computation.7 | async-start | bytes 7520256 | tf_op jit(solution)/shard_map/reduce_scatter | solution.py:250
  220.4 11.6 %slice-start = ((s8[12582912]{0:T(1024)(128)(4,1)}), s8[4194304]{0:T(1024)(128)(4,1)S(1)}, s32[]{:S(2)}) async-start(s8[12582912]{0:T(1024)(128)(4,1)} %bitcast.150), calls=%async_computation.9 | async-start | bytes 8388608 | tf_op jit(solution)/shard_map/while
  220.4 11.6 %slice-start.1 = ((s8[12582912]{0:T(1024)(128)(4,1)}), s8[4194304]{0:T(1024)(128)(4,1)S(1)}, s32[]{:S(2)}) async-start(s8[12582912]{0:T(1024)(128)(4,1)} %bitcast.150), calls=%async_computation.10 | async-start | bytes 8388608 | tf_op jit(solution)/shard_map/while
  220.4 13.2 %slice-start.2 = ((s8[12582912]{0:T(1024)(128)(4,1)}), s8[4194304]{0:T(1024)(128)(4,1)S(1)}, s32[]{:S(2)}) async-start(s8[12582912]{0:T(1024)(128)(4,1)} %bitcast.150), calls=%async_computation.11 | async-start | bytes 8388608 | tf_op jit(solution)/shard_map/while
  220.4 13.2 %copy-start.10 = (pred[512,512]{0,1:T(8,128)(4,1)S(1)}, pred[512,512]{0,1:T(8,128)(4,1)}, u32[]{:S(2)}) copy-start(pred[512,512]{0,1:T(8,128)(4,1)} %broadcast_compare_fusion.5) | copy-start | bytes 786436 | tf_op jit(solution)/shard_map/while
  220.4 13.2 %copy-start.15 = (f32[12,512]{1,0:T(8,128)S(1)}, f32[12,512]{1,0:T(8,128)}, u32[]{:S(2)}) copy-start(f32[12,512]{1,0:T(8,128)} %dynamic-slice_bitcast_fusion.7) | copy-start | bytes 73732 | tf_op jit(solution)/shard_map/while
  264.1 12.1 %slice-start = ((s8[12582912]{0:T(1024)(128)(4,1)}), s8[4194304]{0:T(1024)(128)(4,1)S(1)}, s32[]{:S(2)}) async-start(s8[12582912]{0:T(1024)(128)(4,1)} %bitcast.150), calls=%async_computation.9 | async-start | bytes 8388608 | tf_op jit(solution)/shard_map/while
  264.1 12.1 %slice-start.1 = ((s8[12582912]{0:T(1024)(128)(4,1)}), s8[4194304]{0:T(1024)(128)(4,1)S(1)}, s32[]{:S(2)}) async-start(s8[12582912]{0:T(1024)(128)(4,1)} %bitcast.150), calls=%async_computation.10 | async-start | bytes 8388608 | tf_op jit(solution)/shard_map/while
  264.1 13.8 %slice-start.2 = ((s8[12582912]{0:T(1024)(128)(4,1)}), s8[4194304]{0:T(1024)(128)(4,1)S(1)}, s32[]{:S(2)}) async-start(s8[12582912]{0:T(1024)(128)(4,1)} %bitcast.150), calls=%async_computation.11 | async-start | bytes 8388608 | tf_op jit(solution)/shard_map/while
  264.1 13.8 %copy-start.10 = (pred[512,512]{0,1:T(8,128)(4,1)S(1)}, pred[512,512]{0,1:T(8,128)(4,1)}, u32[]{:S(2)}) copy-start(pred[512,512]{0,1:T(8,128)(4,1)} %broadcast_compare_fusion.5) | copy-start | bytes 786436 | tf_op jit(solution)/shard_map/while
  264.1 13.8 %copy-start.15 = (f32[12,512]{1,0:T(8,128)S(1)}, f32[12,512]{1,0:T(8,128)}, u32[]{:S(2)}) copy-start(f32[12,512]{1,0:T(8,128)} %dynamic-slice_bitcast_fusion.7) | copy-start | bytes 73732 | tf_op jit(solution)/shard_map/while
  310.8 161.1 %copy-start.34 = (f32[1024]{0:T(1024)S(1)}, f32[1024]{0:T(1024)}, u32[]{:S(2)}) copy-start(f32[1024]{0:T(1024)} %copy-done.33) | copy-start | bytes 12292
  310.8 292.0 %all-reduce.14.cloned.1.call-start = ((), (), s32[]{:S(2)}) async-start(), calls=%async_computation.8 | async-start | bytes 1327104 | tf_op jit(solution)/shard_map/psum | solution.py:284
  (59 other events, 242.4 us)
Sparse Core Ops, SparseCore 0:
  180.3 59.3 reduce-scatter.6
  244.4 110.3 reduce-scatter.8
  358.9 111.0 reduce-scatter.10
  474.5 90.3 reduce-scatter.12
  568.3 34.3 all-reduce.13
